TPU v7x, 512 devices: a whole 4x4x16 slice. The times are simulated.
512 devices in a mesh: row: 16 (over y_lo, x, core), col: 32 (over y_hi, z).
Axes of the slice: x: 4, y: 4 (y_hi: 2, y_lo: 2; y = y_hi * 2 + y_lo), z: 16, core: 2. Of those that a mesh axis runs over, the one named last changes fastest.
Arguments:
- amplitudes: float32 [8192, 256], P('row', 'col'), may hold values from -6 to 6
- integrals: float32 [256, 8192], P('row', 'col'), may hold values from -0.375 to 0.375
- occ_counts: int32 [8], replicated, may hold values from 1 to 10, 40 in all
- vir_counts: int32 [8], replicated, may hold values from 1 to 80, 400 in all
Outputs:
- symmetrized: float32 [8192, 8192], P('row', 'col')
Inputs may be any that keep to these rules, and one draw needn't show every extreme that they name: `occ_counts`: counts of occupied orbitals in the 8 irreducible representations, summing to 40. `vir_counts`: counts of virtual orbitals in the 8 irreducible representations, summing to 400.
All inputs are finite; a program needn't handle non-finite values.
Results may differ from a plain program's by a relative error of at most 0.00007.
Values sent between devices are 32-bit elements; how exact they have to be, the bound alone decides.
A program may use at most 64 MiB of HBM per device.

v0:
```python
import jax
import jax.numpy as jnp
from jax import lax
from jax.sharding import PartitionSpec as P

NVIR = 400


def orbital_irreps(orbitals, counts):
    bounds = jnp.cumsum(counts)[:-1]
    return jnp.sum((orbitals[:, None] >= bounds[None, :]).astype(jnp.int32), axis=1)


def pair_labels(positions, occ_counts, vir_counts):
    occ_part = orbital_irreps(positions // NVIR, occ_counts)
    vir_part = orbital_irreps(positions % NVIR, vir_counts)
    return jnp.bitwise_xor(occ_part, vir_part)


def exact_dot(left, right):
    return jnp.dot(left, right, precision=lax.Precision.HIGHEST, preferred_element_type=jnp.float32)


def assemble(received, row_count, narrow):
    grouped = received.reshape(row_count, 2, -1).transpose(1, 0, 2).reshape(2, narrow, narrow)
    return grouped.transpose(1, 0, 2).reshape(narrow, 2 * narrow).T


def per_device(amplitudes, integrals, occ_counts, vir_counts):
    row_count = lax.axis_size("row")
    col_count = lax.axis_size("col")
    row_index = lax.axis_index("row")
    col_index = lax.axis_index("col")
    tall = amplitudes.shape[0]
    narrow = integrals.shape[1]
    row_labels = pair_labels(
        row_index * tall + jnp.arange(tall, dtype=jnp.int32), occ_counts, vir_counts
    )
    col_labels = pair_labels(
        col_index * narrow + jnp.arange(narrow, dtype=jnp.int32), occ_counts, vir_counts
    )
    allowed = row_labels[:, None] == col_labels[None, :]
    parity = col_index % 2
    int_cols = lax.all_gather(integrals, "row", axis=0, tiled=True)
    product = exact_dot(lax.all_gather(amplitudes, "col", axis=1, tiled=True), int_cols)
    flattened = product.reshape(2, row_count, -1)
    oriented = jnp.where(parity == 0, flattened, flattened[::-1])
    outgoing = oriented.transpose(1, 0, 2).reshape(col_count, -1)
    section_one = lax.all_to_all(outgoing, "col", split_axis=0, concat_axis=0, tiled=True)
    section_two = lax.all_to_all(section_one, "row", split_axis=0, concat_axis=0, tiled=True)
    paired = section_two.reshape(row_count, 2, -1)
    paired = jnp.where(parity == 0, paired, paired[:, ::-1]).reshape(col_count, -1)
    section_three = lax.all_to_all(paired, "col", split_axis=0, concat_axis=0, tiled=True)
    arrived = section_three.reshape(row_count, 2, -1)
    arrived = jnp.where(parity == 0, arrived, arrived[:, ::-1]).reshape(col_count, -1)
    mirrored = assemble(arrived, row_count, narrow)
    return jnp.where(allowed, product + mirrored, 0.0)


def solution(mesh):
    placed = (P("row", "col"), P("row", "col"), P(), P())
    return jax.shard_map(
        per_device, mesh=mesh, in_specs=placed, out_specs=P("row", "col"), check_vma=False
    )
```

profile of v0, /device:TPU:32, one launch (start us, length us, event | category | flops | bytes accessed | tf_op | source)
XLA Modules:
  0.0 209.4 jit_solution(9081670944879843364)
XLA Ops:
  0.0 0.7 copy-done
  0.7 81.1 %all_gather.6 = f32[512,256]{0,1:T(8,128)S(1)} all-gather(f32[512,8]{0,1:T(8,128)S(1)} %copy-done), channel_id=1, replica_groups=mesh['row'=16,'col'=32] {'col'}, dimensions={1}, use_global_device_ids=true | all-gather | bytes 540672 | tf_op jit(solution)/shard_map/all_gather | solution.py:45
  81.8 19.5 %all_gather.7 = f32[256,256]{1,0:T(8,128)S(1)} all-gather(f32[16,256]{1,0:T(8,128)S(1)} %copy-done.1), channel_id=1, replica_groups=mesh['row'=16,'col'=32] {'row'}, dimensions={0}, use_global_device_ids=true | all-gather | bytes 278528 | tf_op jit(solution)/shard_map/all_gather | solution.py:44
  101.3 1.0 fusion.8
  102.4 0.4 copy.20
  102.8 1.9 rev.9
  104.7 0.5 select_bitcast_fusion.1
  105.3 0.8 all_to_all.24
  106.1 41.9 %all_to_all.29 = f32[32,1,4096]{2,1,0:T(1,128)S(1)} all-to-all(f32[32,1,4096]{2,1,0:T(1,128)S(1)} %all_to_all.24), channel_id=1, replica_groups=mesh['row'=16,'col'=32] {'col'}, dimensions={0} | all-to-all | bytes 1048576 | tf_op jit(solution)/shard_map/all_to_all | solution.py:49
  147.9 1.2 reduce
  149.2 0.3 all_to_all.20
  149.5 13.5 %all_to_all.30 = f32[16,2,4096]{2,1,0:T(2,128)S(1)} all-to-all(f32[16,2,4096]{2,1,0:T(2,128)S(1)} %all_to_all.20), channel_id=1, replica_groups=mesh['row'=16,'col'=32] {'row'}, dimensions={0} | all-to-all | bytes 1048576 | tf_op jit(solution)/shard_map/all_to_all | solution.py:50
  163.0 1.9 rev.10
  164.9 1.6 all_to_all.25
  166.5 4.5 %all-to-all-start.2 = ((f32[32,1,4096]{2,1,0:T(1,128)}), f32[32,1,4096]{2,1,0:T(1,128)S(1)}, u32[]{:S(2)}, u32[]{:S(2)}) async-start(f32[32,1,4096]{2,1,0:T(1,128)} %all_to_all.25), calls=%async_computation.2 | async-start | bytes 1048576 | tf_op jit(solution)/shard_map/all_to_all | solution.py:53
  171.1 0.6 copy-done.2
  171.9 0.7 copy-done.3
  173.2 30.9 %all-to-all-done.2 = f32[32,1,4096]{2,1,0:T(1,128)S(1)} async-done(((f32[32,1,4096]{2,1,0:T(1,128)}), f32[32,1,4096]{2,1,0:T(1,128)S(1)}, u32[]{:S(2)}, u32[]{:S(2)}) %all-to-all-start.2) | async-done | bytes 524320 | tf_op jit(solution)/shard_map/all_to_all | solution.py:53
  204.1 1.2 reduce.1
  205.3 0.3 reshape.89
  205.6 1.9 rev.11
  207.5 0.3 select_bitcast_fusion
  207.8 0.3 copy.23
  208.5 0.9 fusion
  (21 shorter events, 1.2 us)
Async XLA Ops:
  0.0 0.7 copy-start
  0.7 81.1 %copy-start.1 = (f32[16,256]{1,0:T(8,128)S(1)}, f32[16,256]{1,0:T(8,128)}, u32[]{:S(2)}) copy-start(f32[16,256]{1,0:T(8,128)} %param.5) | copy-start | bytes 49156
  166.5 37.5 %all-to-all-start.2 = ((f32[32,1,4096]{2,1,0:T(1,128)}), f32[32,1,4096]{2,1,0:T(1,128)S(1)}, u32[]{:S(2)}, u32[]{:S(2)}) async-start(f32[32,1,4096]{2,1,0:T(1,128)} %all_to_all.25), calls=%async_computation.2 | async-start | bytes 1048576 | tf_op jit(solution)/shard_map/all_to_all | solution.py:53
  171.1 0.7 copy-start.2
  171.9 0.7 copy-start.3
where the time goes:
time: 210 us; the launch traced here: 209 us
  blocking collectives  156 us (74%)
  waiting for transfers between devices  30.9 us (15%)
  local copies, waits for them, and re-layouts  11.9 us (6%)
  other arithmetic  5.09 us (2%)
  starting transfers between devices  4.54 us (2%)
    all_gather x1, blocking collectives, per_device(): lax.all_gather(amplitudes, 'col', axis=1, tiled=True)  81.1 us
    all_to_all x1, blocking collectives, per_device(): lax.all_to_all(outgoing, 'col', split_axis=0, concat_axis=0, tiled=True)  41.9 us
    all_to_all x1, waiting for transfers between devices, per_device(): lax.all_to_all(paired, 'col', split_axis=0, concat_axis=0, tiled=True)  30.9 us
    all_gather x1, blocking collectives, per_device(): int_cols = lax.all_gather(integrals, 'row', axis=0, tiled=True)  19.5 us
    all_to_all x1, blocking collectives, per_device(): lax.all_to_all(section_one, 'row', split_axis=0, concat_axis=0, tiled=True)  13.5 us
    all_to_all x1, starting transfers between devices, per_device(): lax.all_to_all(paired, 'col', split_axis=0, concat_axis=0, tiled=True)  4.54 us
  transfers between devices with their start and end apart: 1, of which 1 were waited for; matrix products, arithmetic and copies ran while one was open for 0% of the time, Pallas kernels for 0%

commit v1 on v0

--- a/solution.py
+++ b/solution.py
@@ -4,6 +4,11 @@
 from jax.sharding import PartitionSpec as P
 
 NVIR = 400
+
+
+def swapped_in(array, axis, dim):
+    outgoing = jnp.stack([array] * lax.axis_size(axis))
+    return jnp.concatenate(lax.all_to_all(outgoing, axis, 0, 0), axis=dim)
 
 
 def orbital_irreps(orbitals, counts):
@@ -41,7 +46,7 @@
     )
     allowed = row_labels[:, None] == col_labels[None, :]
     parity = col_index % 2
-    int_cols = lax.all_gather(integrals, "row", axis=0, tiled=True)
+    int_cols = swapped_in(integrals, "row", 0)
     product = exact_dot(lax.all_gather(amplitudes, "col", axis=1, tiled=True), int_cols)
     flattened = product.reshape(2, row_count, -1)
     oriented = jnp.where(parity == 0, flattened, flattened[::-1])

time: 210 us -> 190 us (0.905)
  blocking collectives: 156 us -> 129 us
  starting transfers between devices: 4.54 us -> 10.2 us
    all_gather x1 -> x0, blocking collectives: 19.5 us -> none  [per_device(): int_cols = lax.all_gather(integrals, 'row', axis=0, tiled=True)]
    all_to_all x1, blocking collectives: 41.9 us -> 30.8 us  [per_device(): lax.all_to_all(outgoing, 'col', split_axis=0, concat_axis=0, tiled=True)]
    all_to_all x0 -> x1, starting transfers between devices: none -> 5.42 us  [swapped_in(): return jnp.concatenate(lax.all_to_all(outgoing, axis, 0, 0), axis=dim)]
    all_to_all x1, blocking collectives: 13.5 us -> 17.6 us  [per_device(): lax.all_to_all(section_one, 'row', split_axis=0, concat_axis=0, tiled=True)]
  transfers between devices with their start and end apart: 1 -> 2, of which waited for: 1 -> 1; matrix products, arithmetic and copies ran while one was open for 0% -> 0% of each run, Pallas kernels for 0% -> 0%
where the time goes in v1:
time: 190 us
  blocking collectives  129 us (68%)
  waiting for transfers between devices  30.9 us (16%)
  local copies, waits for them, and re-layouts  13.3 us (7%)
  starting transfers between devices  10.2 us (5%)
  other arithmetic  5.09 us (3%)
    all_gather x1, blocking collectives, per_device(): lax.all_gather(amplitudes, 'col', axis=1, tiled=True)  80.6 us
    all_to_all x1, waiting for transfers between devices, per_device(): lax.all_to_all(paired, 'col', split_axis=0, concat_axis=0, tiled=True)  30.9 us
    all_to_all x1, blocking collectives, per_device(): lax.all_to_all(outgoing, 'col', split_axis=0, concat_axis=0, tiled=True)  30.8 us
    all_to_all x1, blocking collectives, per_device(): lax.all_to_all(section_one, 'row', split_axis=0, concat_axis=0, tiled=True)  17.6 us
    all_to_all x1, starting transfers between devices, swapped_in(): return jnp.concatenate(lax.all_to_all(outgoing, axis, 0, 0), axis=dim)  5.42 us
    all_to_all x1, starting transfers between devices, per_device(): lax.all_to_all(paired, 'col', split_axis=0, concat_axis=0, tiled=True)  4.73 us
  transfers between devices with their start and end apart: 2, of which 1 were waited for; matrix products, arithmetic and copies ran while one was open for 0% of the time, Pallas kernels for 0%

profile of v1, /device:TPU:32, one launch (start us, length us, event | category | flops | bytes accessed | tf_op | source)
XLA Modules:
  0.0 189.6 jit_solution(1494604112932603913)
XLA Ops:
  0.0 1.4 stack.2
  1.4 5.4 %all-to-all-start = ((f32[16,16,256]{2,1,0:T(8,128)}), f32[16,16,256]{2,1,0:T(8,128)S(1)}, u32[]{:S(2)}, u32[]{:S(2)}) async-start(f32[16,16,256]{2,1,0:T(8,128)} %stack.2), calls=%async_computation | async-start | bytes 524288 | tf_op jit(solution)/shard_map/all_to_all | solution.py:11
  6.9 0.7 copy-done
  7.6 80.6 %all_gather.3 = f32[512,256]{0,1:T(8,128)S(1)} all-gather(f32[512,8]{0,1:T(8,128)S(1)} %copy-done), channel_id=1, replica_groups=mesh['row'=16,'col'=32] {'col'}, dimensions={1}, use_global_device_ids=true | all-gather | bytes 540672 | tf_op jit(solution)/shard_map/all_gather | solution.py:50
  88.2 1.0 fusion.8
  89.3 0.4 copy.20
  89.8 1.9 %rev.9 = f32[2,16,4096]{2,0,1:T(2,128)S(1)} reverse(f32[2,16,4096]{2,0,1:T(2,128)S(1)} %copy.20), dimensions={0} | reverse | bytes 1048576 | tf_op jit(solution)/shard_map/rev | solution.py:52
  91.7 0.5 select_bitcast_fusion.1
  92.2 0.8 all_to_all.28
  93.0 30.8 %all_to_all.34 = f32[32,1,4096]{2,1,0:T(1,128)S(1)} all-to-all(f32[32,1,4096]{2,1,0:T(1,128)S(1)} %all_to_all.28), channel_id=1, replica_groups=mesh['row'=16,'col'=32] {'col'}, dimensions={0} | all-to-all | bytes 1048576 | tf_op jit(solution)/shard_map/all_to_all | solution.py:54
  123.8 1.2 reduce
  125.1 0.3 all_to_all.24
  125.4 17.6 %all_to_all.35 = f32[16,2,4096]{2,1,0:T(2,128)S(1)} all-to-all(f32[16,2,4096]{2,1,0:T(2,128)S(1)} %all_to_all.24), channel_id=1, replica_groups=mesh['row'=16,'col'=32] {'row'}, dimensions={0} | all-to-all | bytes 1048576 | tf_op jit(solution)/shard_map/all_to_all | solution.py:55
  143.0 1.9 rev.10
  145.0 1.6 all_to_all.29
  146.6 4.7 %all-to-all-start.3 = ((f32[32,1,4096]{2,1,0:T(1,128)}), f32[32,1,4096]{2,1,0:T(1,128)S(1)}, u32[]{:S(2)}, u32[]{:S(2)}) async-start(f32[32,1,4096]{2,1,0:T(1,128)} %all_to_all.29), calls=%async_computation.3 | async-start | bytes 1048576 | tf_op jit(solution)/shard_map/all_to_all | solution.py:58
  151.3 0.6 copy-done.1
  152.1 0.7 copy-done.2
  153.4 30.9 %all-to-all-done.3 = f32[32,1,4096]{2,1,0:T(1,128)S(1)} async-done(((f32[32,1,4096]{2,1,0:T(1,128)}), f32[32,1,4096]{2,1,0:T(1,128)S(1)}, u32[]{:S(2)}, u32[]{:S(2)}) %all-to-all-start.3) | async-done | bytes 524320 | tf_op jit(solution)/shard_map/all_to_all | solution.py:58
  184.3 1.2 reduce.1
  185.8 1.9 %rev.11 = f32[16,2,4096]{2,1,0:T(2,128)S(1)} reverse(f32[16,2,4096]{2,1,0:T(2,128)S(1)} %reshape.95), dimensions={1} | reverse | bytes 1048576 | tf_op jit(solution)/shard_map/rev | solution.py:60
  187.7 0.3 select_bitcast_fusion
  188.1 0.3 copy.23
  188.7 0.9 fusion
  (21 shorter events, 1.5 us)
Async XLA Ops:
  1.4 86.8 %all-to-all-start = ((f32[16,16,256]{2,1,0:T(8,128)}), f32[16,16,256]{2,1,0:T(8,128)S(1)}, u32[]{:S(2)}, u32[]{:S(2)}) async-start(f32[16,16,256]{2,1,0:T(8,128)} %stack.2), calls=%async_computation | async-start | bytes 524288 | tf_op jit(solution)/shard_map/all_to_all | solution.py:11
  6.9 0.7 copy-start
  146.6 37.7 %all-to-all-start.3 = ((f32[32,1,4096]{2,1,0:T(1,128)}), f32[32,1,4096]{2,1,0:T(1,128)S(1)}, u32[]{:S(2)}, u32[]{:S(2)}) async-start(f32[32,1,4096]{2,1,0:T(1,128)} %all_to_all.29), calls=%async_computation.3 | async-start | bytes 1048576 | tf_op jit(solution)/shard_map/all_to_all | solution.py:58
  151.3 0.7 copy-start.1
  152.1 0.7 copy-start.2
